TPU v7x, 256 devices: a whole 4x4x8 slice. The times are simulated.
256 devices in a mesh: seq: 64 (over y, x_lo, z), head: 4 (over x_hi, core).
Axes of the slice: x: 4 (x_hi: 2, x_lo: 2; x = x_hi * 2 + x_lo), y: 4, z: 8, core: 2. Of those that a mesh axis runs over, the one named last changes fastest.
Arguments:
- query_raw: bfloat16 [32768, 4096], P('seq', 'head'), may hold values from -600 to 600
- key_before_norm: bfloat16 [32768, 2048], P('seq', 'head'), may hold values from -600 to 600
- value_input: bfloat16 [32768, 2048], P('seq', 'head'), may hold values from -6 to 6
- out_cotangent: bfloat16 [32768, 4096], P('seq', 'head'), may hold values from -6 to 6
- query_gain: float32 [128], replicated, may hold values from 0.5 to 7
- key_norm_gain: float32 [128], replicated, may hold values from 0.5 to 7
- doc_starts: int32 [4, 8], replicated, may hold values from 0 to 8191, as said below
- windows: int32 [4], replicated, may hold values from 513 to 1024, as said below
Outputs:
- query_gradient: bfloat16 [32768, 4096], P('seq', 'head')
- key_gradient: bfloat16 [32768, 2048], P('seq', 'head')
- value_gradient: bfloat16 [32768, 2048], P('seq', 'head')
- query_norm_gain_gradient: float32 [128], replicated
- key_norm_gain_gradient: float32 [128], replicated
Inputs may be any that keep to these rules, and one draw needn't show every extreme that they name: `doc_starts`: each row begins with 0 and rises strictly; no document starts at position 4096. `windows`: some sequence has a window of exactly 1024.
All inputs are finite; a program needn't handle non-finite values.
Results may differ from a plain program's by a relative error of at most 0.025.
The roundings to bfloat16 on the way count: a program that leaves them out, or rounds other values in their place, can miss the bound.
Values may be sent and summed in bfloat16 or wider, within the bound.
A program may use at most 128 MiB of HBM per device.

v0:
```python
import jax
import jax.numpy as jnp
from jax import lax
from jax.sharding import PartitionSpec as P

WINDOW = 1024
SLABS = 4


score_scale = 168.0 ** (-0.5)
norm_eps = 1e-06
masked_score = -1e30


def from_behind(shard, axis, by):
    peers = lax.axis_size(axis)
    return lax.ppermute(shard, axis, [(i, (i + by) % peers) for i in range(peers)])


def token_info(token_ids, doc_starts, windows, slab_length, total_tokens):
    placed = (token_ids + total_tokens - slab_length // 2) % total_tokens
    slab_id = placed // slab_length
    in_slab = placed - slab_id * slab_length
    one_hot = (jnp.arange(windows.shape[0], dtype=jnp.int32)[None, :] == slab_id[:, None]).astype(
        jnp.int32
    )
    row_starts = jnp.sum(one_hot[:, :, None] * doc_starts[None, :, :], axis=1)
    reached = row_starts <= in_slab[:, None]
    doc_count = jnp.sum(reached.astype(jnp.int32), axis=1)
    doc_begin = jnp.max(jnp.where(reached, row_starts, 0), axis=1)
    doc_id = slab_id * doc_starts.shape[1] + doc_count
    win_size = jnp.sum(one_hot * windows[None, :], axis=1)
    return (doc_id, in_slab, in_slab - doc_begin, win_size)


def visible_pairs(query_doc, query_slab, query_window, key_doc, key_slab):
    pos_gap = query_slab[:, None] - key_slab[None, :]
    return (
        (query_doc[:, None] == key_doc[None, :])
        & (pos_gap >= 0)
        & (pos_gap < query_window[:, None])
    )


def rope_tables(rope_pos, head_dim):
    half_dim = head_dim // 2
    spacing = jnp.arange(half_dim, dtype=jnp.float32) * (2.0 / head_dim)
    inverse_freq = 10000.0 ** (-spacing)
    angle = rope_pos.astype(jnp.float32)[:, None] * inverse_freq[None, :]
    return (jnp.cos(angle)[:, None, :], jnp.sin(angle)[:, None, :])


def apply_norm(raw_rows, gain_vec, cosine_table, sine_table):
    floats = raw_rows.astype(jnp.float32)
    inverse = lax.rsqrt(jnp.mean(floats * floats, axis=-1) + norm_eps)
    scaled = floats * inverse[..., None] * gain_vec
    half_dim = scaled.shape[-1] // 2
    low_half, high_half = (scaled[..., :half_dim], scaled[..., half_dim:])
    turned = jnp.concatenate(
        [
            low_half * cosine_table - high_half * sine_table,
            high_half * cosine_table + low_half * sine_table,
        ],
        axis=-1,
    )
    return (turned.astype(jnp.bfloat16), floats, inverse)


def norm_backward(grad_hat, floats, inverse, gain_vec, cosine_table, sine_table):
    half_dim = grad_hat.shape[-1] // 2
    low_half, high_half = (grad_hat[..., :half_dim], grad_hat[..., half_dim:])
    grad_scaled = jnp.concatenate(
        [
            low_half * cosine_table + high_half * sine_table,
            high_half * cosine_table - low_half * sine_table,
        ],
        axis=-1,
    )
    unit_rows = floats * inverse[..., None]
    gain_grad = jnp.sum(grad_scaled * unit_rows, axis=(0, 1))
    weighted = grad_scaled * gain_vec
    correction = jnp.mean(weighted * floats, axis=-1)
    grad_raw = (
        inverse[..., None] * weighted
        - floats * (inverse * inverse * inverse * correction)[..., None]
    )
    return (grad_raw, gain_grad)


def to_groups(head_rows, key_heads, group_width):
    shard_rows, query_heads, head_dim = head_rows.shape
    grouped = head_rows.reshape(shard_rows, key_heads, group_width, head_dim)
    return jnp.transpose(grouped, (1, 2, 0, 3))


def head_forward(query_group, grad_group, key_block, value_block, visible):
    scores = (
        jnp.einsum("grd,kd->grk", query_group, key_block, preferred_element_type=jnp.float32)
        * score_scale
    )
    scores = jnp.where(visible[None], scores, masked_score)
    row_max = jnp.max(scores, axis=-1, keepdims=True)
    exponent = jnp.exp(scores - row_max)
    row_sum = jnp.sum(exponent, axis=-1, keepdims=True)
    softmax = exponent / row_sum
    grad_soft = jnp.einsum(
        "grd,kd->grk", grad_group, value_block, preferred_element_type=jnp.float32
    )
    row_delta = jnp.sum(softmax * grad_soft, axis=-1, keepdims=True)
    grad_scores = (softmax * (grad_soft - row_delta)).astype(jnp.bfloat16)
    return (softmax.astype(jnp.bfloat16), grad_scores, row_max, row_sum, row_delta)


def shards(
    query_raw,
    key_before_norm,
    value_input,
    out_cotangent,
    query_gain,
    key_norm_gain,
    doc_starts,
    windows,
):
    shard_rows = query_raw.shape[0]
    head_dim = query_gain.shape[0]
    key_heads = key_before_norm.shape[1] // head_dim
    query_heads = query_raw.shape[1] // head_dim
    group_width = query_heads // key_heads
    shard_count = lax.axis_size("seq")
    total_rows = shard_count * shard_rows
    slab_length = total_rows // SLABS
    reach_shards = (WINDOW - 1) // shard_rows + 1
    shard_index = lax.axis_index("seq")
    offsets = jnp.arange(shard_rows, dtype=jnp.int32)

    def info_of(source_index):
        return token_info(
            source_index * shard_rows + offsets, doc_starts, windows, slab_length, total_rows
        )

    own_doc, own_slab, own_rope, own_window = info_of(shard_index)
    cosine_table, sine_table = rope_tables(own_rope, head_dim)
    query_unit, query_float, query_inverse = apply_norm(
        query_raw.reshape(shard_rows, query_heads, head_dim), query_gain, cosine_table, sine_table
    )
    key_unit, key_single, key_inverse_norm = apply_norm(
        key_before_norm.reshape(shard_rows, key_heads, head_dim),
        key_norm_gain,
        cosine_table,
        sine_table,
    )
    value_row_block = value_input.reshape(shard_rows, key_heads, head_dim)
    gradient_rows = out_cotangent.reshape(shard_rows, query_heads, head_dim)
    key_sequence_list = [key_unit]
    value_list = [value_row_block]
    doc_list = [own_doc]
    slab_list = [own_slab]
    for distance in range(1, reach_shards + 1):
        far_key, far_value = from_behind((key_unit, value_row_block), "seq", distance)
        far_doc, far_slab, far_rope, far_window = info_of((shard_index - distance) % shard_count)
        key_sequence_list.append(far_key)
        value_list.append(far_value)
        doc_list.append(far_doc)
        slab_list.append(far_slab)
    keys_heads = jnp.transpose(jnp.concatenate(key_sequence_list, 0), (1, 0, 2))
    values_heads = jnp.transpose(jnp.concatenate(value_list, 0), (1, 0, 2))
    visible = visible_pairs(
        own_doc, own_slab, own_window, jnp.concatenate(doc_list, 0), jnp.concatenate(slab_list, 0)
    )
    query_groups = to_groups(query_unit, key_heads, group_width)
    grad_groups = to_groups(gradient_rows, key_heads, group_width)

    def per_head(operands):
        query_group, grad_group, key_block, value_block = operands
        soft_half, grad_scores, row_max, row_sum, row_delta = head_forward(
            query_group, grad_group, key_block, value_block, visible
        )
        grad_query = score_scale * jnp.einsum(
            "grk,kd->grd", grad_scores, key_block, preferred_element_type=jnp.float32
        )
        grad_key = score_scale * jnp.einsum(
            "grk,grd->kd", grad_scores, query_group, preferred_element_type=jnp.float32
        )
        grad_value = jnp.einsum(
            "grk,grd->kd", soft_half, grad_group, preferred_element_type=jnp.float32
        )
        return (grad_query, grad_key, grad_value)

    grad_query, key_all, value_all = lax.map(
        per_head, (query_groups, grad_groups, keys_heads, values_heads)
    )
    grad_key = key_all[:, :shard_rows]
    grad_value = value_all[:, :shard_rows]
    for distance in range(1, reach_shards + 1):
        lower = distance * shard_rows
        back_key, back_value = from_behind(
            (key_all[:, lower : lower + shard_rows], value_all[:, lower : lower + shard_rows]),
            "seq",
            -distance,
        )
        grad_key = grad_key + back_key
        grad_value = grad_value + back_value
    grad_query_hat = jnp.transpose(grad_query, (2, 0, 1, 3)).reshape(
        shard_rows, query_heads, head_dim
    )
    grad_key_hat = jnp.transpose(grad_key, (1, 0, 2))
    query_gradient, query_gain_part = norm_backward(
        grad_query_hat, query_float, query_inverse, query_gain, cosine_table, sine_table
    )
    key_gradient, key_gain_part = norm_backward(
        grad_key_hat, key_single, key_inverse_norm, key_norm_gain, cosine_table, sine_table
    )
    query_norm_gain_gradient, key_norm_gain_gradient = lax.psum(
        (query_gain_part, key_gain_part), ("seq", "head")
    )
    value_gradient = (
        jnp.transpose(grad_value, (1, 0, 2))
        .reshape(shard_rows, key_heads * head_dim)
        .astype(jnp.bfloat16)
    )
    return (
        query_gradient.reshape(shard_rows, query_heads * head_dim).astype(jnp.bfloat16),
        key_gradient.reshape(shard_rows, key_heads * head_dim).astype(jnp.bfloat16),
        value_gradient,
        query_norm_gain_gradient,
        key_norm_gain_gradient,
    )


def solution(mesh):
    placed = (
        P("seq", "head"),
        P("seq", "head"),
        P("seq", "head"),
        P("seq", "head"),
        P(),
        P(),
        P(),
        P(),
    )
    return jax.shard_map(
        shards,
        mesh=mesh,
        in_specs=placed,
        out_specs=(P("seq", "head"), P("seq", "head"), P("seq", "head"), P(), P()),
        check_vma=False,
    )
```

profile of v0, /device:TPU:2, one launch (start us, length us, event | category | flops | bytes accessed | tf_op | source)
XLA Modules:
  0.0 372.0 jit_solution(18229699175735696365)
XLA Ops:
  1.6 1.4 reshape.318
  7.5 1.9 collective-permute-start
  9.4 3.3 collective-permute-start.1
  13.7 3.1 collective-permute-start.2
  16.8 1.5 collective-permute-start.3
  22.4 1.5 maximum_bitcast_fusion.2
  24.9 2.3 copy.126
  27.2 22.7 %collective-permute-done.1 = bf16[512,4,128]{2,0,1:T(8,128)(2,1)} collective-permute-done((bf16[512,4,128]{2,0,1:T(8,128)(2,1)}, bf16[512,4,128]{2,0,1:T(8,128)(2,1)}, u32[]{:S(2)}, u32[]{:S(2)}) %collective-permute-start.1) | collective-permute-done | bytes 524320 | tf_op jit(solution)/shard_map/ppermute | solution.py:17
  49.9 2.9 maximum_bitcast_fusion
  52.7 7.8 %collective-permute-done.2 = bf16[512,4,128]{0,2,1:T(8,128)(2,1)} collective-permute-done((bf16[512,4,128]{0,2,1:T(8,128)(2,1)}, bf16[512,4,128]{0,2,1:T(8,128)(2,1)}, u32[]{:S(2)}, u32[]{:S(2)}) %collective-permute-start.2) | collective-permute-done | bytes 524320 | tf_op jit(solution)/shard_map/ppermute | solution.py:17
  60.6 12.3 %collective-permute-done.3 = bf16[512,4,128]{0,2,1:T(8,128)(2,1)} collective-permute-done((bf16[512,4,128]{0,2,1:T(8,128)(2,1)}, bf16[512,4,128]{0,2,1:T(8,128)(2,1)}, u32[]{:S(2)}, u32[]{:S(2)}) %collective-permute-start.3) | collective-permute-done | bytes 524320 | tf_op jit(solution)/shard_map/ppermute | solution.py:17
  72.9 2.6 maximum_bitcast_fusion.1
  75.5 97.8 %while.15 = (s32[]{:T(128)}, f32[4,2,512,128]{3,2,1,0:T(8,128)}, f32[4,1536,128]{2,1,0:T(8,128)}, f32[4,1536,128]{2,1,0:T(8,128)}, bf16[4,2,512,128]{3,2,1,0:T(8...) while((s32[]{:T(128)}, f32[4,2,512,128]{3,2,1,0:T(8,128)}, ...), condition=%wide.region_14.15_spmd.clone, body=%wide.region_10.14_spmd.clone.sunk | while | flops 2446134272 | bytes 67158200 | solution.py:189
  75.5 1.3 fusion.132
  76.9 6.1 %fusion.133 = (f32[2,512]{1,0:T(2,128)S(1)}, f32[2,512,1536]{2,1,0:T(8,128)}) fusion(pred[512,1536]{1,0:T(8,128)(4,1)S(1)} %fusion.132, bf16[4,1536,128]{2,1,0:T(8,128)(2,1)} %get-tuple-element.355, s32[]{:T(128)} %get-tuple-element.336, bf16[4,2,512,128]{3,2,1,0:T(8,128)(2,1)} %get-tuple-element.354), kind=kOutput, calls=%fused_computation.171.clone.1 | convolution fusion | flops 408946176 | bytes 7738368 | tf_op jit(solution)/shard_map/while/body/eval_jaxpr/sub | solution.py:103
  83.0 4.2 %multiply_reduce_fusion.8 = (f32[2,512]{1,0:T(2,128)S(1)}, f32[2,512,1536]{2,1,0:T(8,128)S(1)}) fusion(f32[2,512,1536]{2,1,0:T(8,128)} %get-tuple-element.318, f32[2,512]{1,0:T(2,128)S(1)} %get-tuple-element.319, bf16[4,1536,128]{1,2,0:T(8,128)(2,1)} %get-tuple-element.357, s32[]{:T(128)} %get-tuple-element.336, ...), kind=kOutput, calls=%fused_computation.3.clone.1 | convolution fusion | flops 407370752 | bytes 13247488 | tf_op jit(solution)/shard_map/while/body/eval_jaxpr/grd,kd->grk/dot_general | solution.py:106
  88.9 2.9 fusion.135
  91.8 2.8 fusion.134
  94.6 5.4 %fusion.136 = f32[4,1536,128]{2,1,0:T(8,128)} fusion(f32[4,1536,128]{2,1,0:T(8,128)} %get-tuple-element.339, s32[]{:T(128)} %get-tuple-element.336, bf16[4,2,512,128]{2,3,1,0:T(8,128)(2,1)} %get-tuple-element.356, f32[2,512]{1,0:T(2,128)S(1)} %get-tuple-element.319, pred[512,1536]{1,0:T(8,128)(4,1)S(1)} %fusion.132, ...), kind=kOutput, calls=%fused_computation.22.clone.1 | convolution fusion | flops 813173248 | bytes 2496512 | tf_op jit(solution)/shard_map/while/body/eval_jaxpr/grk,grd->kd/dot_general | solution.py:184
  99.9 1.3 fusion.132
  101.3 6.1 %fusion.133 = (f32[2,512]{1,0:T(2,128)S(1)}, f32[2,512,1536]{2,1,0:T(8,128)}) fusion(pred[512,1536]{1,0:T(8,128)(4,1)S(1)} %fusion.132, bf16[4,1536,128]{2,1,0:T(8,128)(2,1)} %get-tuple-element.355, s32[]{:T(128)} %get-tuple-element.336, bf16[4,2,512,128]{3,2,1,0:T(8,128)(2,1)} %get-tuple-element.354), kind=kOutput, calls=%fused_computation.171.clone.1 | convolution fusion | flops 408946176 | bytes 7738368 | tf_op jit(solution)/shard_map/while/body/eval_jaxpr/sub | solution.py:103
  107.4 4.2 %multiply_reduce_fusion.8 = (f32[2,512]{1,0:T(2,128)S(1)}, f32[2,512,1536]{2,1,0:T(8,128)S(1)}) fusion(f32[2,512,1536]{2,1,0:T(8,128)} %get-tuple-element.318, f32[2,512]{1,0:T(2,128)S(1)} %get-tuple-element.319, bf16[4,1536,128]{1,2,0:T(8,128)(2,1)} %get-tuple-element.357, s32[]{:T(128)} %get-tuple-element.336, ...), kind=kOutput, calls=%fused_computation.3.clone.1 | convolution fusion | flops 407370752 | bytes 13247488 | tf_op jit(solution)/shard_map/while/body/eval_jaxpr/grd,kd->grk/dot_general | solution.py:106
  113.3 2.9 fusion.135
  116.2 2.8 fusion.134
  119.0 5.4 %fusion.136 = f32[4,1536,128]{2,1,0:T(8,128)} fusion(f32[4,1536,128]{2,1,0:T(8,128)} %get-tuple-element.339, s32[]{:T(128)} %get-tuple-element.336, bf16[4,2,512,128]{2,3,1,0:T(8,128)(2,1)} %get-tuple-element.356, f32[2,512]{1,0:T(2,128)S(1)} %get-tuple-element.319, pred[512,1536]{1,0:T(8,128)(4,1)S(1)} %fusion.132, ...), kind=kOutput, calls=%fused_computation.22.clone.1 | convolution fusion | flops 813173248 | bytes 2496512 | tf_op jit(solution)/shard_map/while/body/eval_jaxpr/grk,grd->kd/dot_general | solution.py:184
  125.8 6.1 %fusion.133 = (f32[2,512]{1,0:T(2,128)S(1)}, f32[2,512,1536]{2,1,0:T(8,128)}) fusion(pred[512,1536]{1,0:T(8,128)(4,1)S(1)} %fusion.132, bf16[4,1536,128]{2,1,0:T(8,128)(2,1)} %get-tuple-element.355, s32[]{:T(128)} %get-tuple-element.336, bf16[4,2,512,128]{3,2,1,0:T(8,128)(2,1)} %get-tuple-element.354), kind=kOutput, calls=%fused_computation.171.clone.1 | convolution fusion | flops 408946176 | bytes 7738368 | tf_op jit(solution)/shard_map/while/body/eval_jaxpr/sub | solution.py:103
  131.9 4.2 %multiply_reduce_fusion.8 = (f32[2,512]{1,0:T(2,128)S(1)}, f32[2,512,1536]{2,1,0:T(8,128)S(1)}) fusion(f32[2,512,1536]{2,1,0:T(8,128)} %get-tuple-element.318, f32[2,512]{1,0:T(2,128)S(1)} %get-tuple-element.319, bf16[4,1536,128]{1,2,0:T(8,128)(2,1)} %get-tuple-element.357, s32[]{:T(128)} %get-tuple-element.336, ...), kind=kOutput, calls=%fused_computation.3.clone.1 | convolution fusion | flops 407370752 | bytes 13247488 | tf_op jit(solution)/shard_map/while/body/eval_jaxpr/grd,kd->grk/dot_general | solution.py:106
  137.8 2.9 fusion.135
  140.7 2.8 fusion.134
  143.5 5.4 %fusion.136 = f32[4,1536,128]{2,1,0:T(8,128)} fusion(f32[4,1536,128]{2,1,0:T(8,128)} %get-tuple-element.339, s32[]{:T(128)} %get-tuple-element.336, bf16[4,2,512,128]{2,3,1,0:T(8,128)(2,1)} %get-tuple-element.356, f32[2,512]{1,0:T(2,128)S(1)} %get-tuple-element.319, pred[512,1536]{1,0:T(8,128)(4,1)S(1)} %fusion.132, ...), kind=kOutput, calls=%fused_computation.22.clone.1 | convolution fusion | flops 813173248 | bytes 2496512 | tf_op jit(solution)/shard_map/while/body/eval_jaxpr/grk,grd->kd/dot_general | solution.py:184
  148.8 1.3 fusion.132
  150.2 6.2 %fusion.133 = (f32[2,512]{1,0:T(2,128)S(1)}, f32[2,512,1536]{2,1,0:T(8,128)}) fusion(pred[512,1536]{1,0:T(8,128)(4,1)S(1)} %fusion.132, bf16[4,1536,128]{2,1,0:T(8,128)(2,1)} %get-tuple-element.355, s32[]{:T(128)} %get-tuple-element.336, bf16[4,2,512,128]{3,2,1,0:T(8,128)(2,1)} %get-tuple-element.354), kind=kOutput, calls=%fused_computation.171.clone.1 | convolution fusion | flops 408946176 | bytes 7738368 | tf_op jit(solution)/shard_map/while/body/eval_jaxpr/sub | solution.py:103
  156.4 4.2 %multiply_reduce_fusion.8 = (f32[2,512]{1,0:T(2,128)S(1)}, f32[2,512,1536]{2,1,0:T(8,128)S(1)}) fusion(f32[2,512,1536]{2,1,0:T(8,128)} %get-tuple-element.318, f32[2,512]{1,0:T(2,128)S(1)} %get-tuple-element.319, bf16[4,1536,128]{1,2,0:T(8,128)(2,1)} %get-tuple-element.357, s32[]{:T(128)} %get-tuple-element.336, ...), kind=kOutput, calls=%fused_computation.3.clone.1 | convolution fusion | flops 407370752 | bytes 13247488 | tf_op jit(solution)/shard_map/while/body/eval_jaxpr/grd,kd->grk/dot_general | solution.py:106
  162.2 3.0 fusion.135
  165.2 2.8 fusion.134
  168.0 5.4 %fusion.136 = f32[4,1536,128]{2,1,0:T(8,128)} fusion(f32[4,1536,128]{2,1,0:T(8,128)} %get-tuple-element.339, s32[]{:T(128)} %get-tuple-element.336, bf16[4,2,512,128]{2,3,1,0:T(8,128)(2,1)} %get-tuple-element.356, f32[2,512]{1,0:T(2,128)S(1)} %get-tuple-element.319, pred[512,1536]{1,0:T(8,128)(4,1)S(1)} %fusion.132, ...), kind=kOutput, calls=%fused_computation.22.clone.1 | convolution fusion | flops 813173248 | bytes 2496512 | tf_op jit(solution)/shard_map/while/body/eval_jaxpr/grk,grd->kd/dot_general | solution.py:184
  173.3 3.2 fusion.102
  176.5 11.0 %collective-permute-start.4 = (f32[4,512,128]{2,1,0:T(8,128)}, f32[4,512,128]{2,1,0:T(8,128)}, u32[]{:S(2)}, u32[]{:S(2)}) collective-permute-start(f32[4,512,128]{2,1,0:T(8,128)} %get-tuple-element.213), channel_id=1, source_target_pairs={{0,252},{4,0},{8,4},{12,8},{16,12},{20,16},{24,20},{28,24},{32,28}... | collective-permute-start | bytes 3145736 | tf_op jit(solution)/shard_map/ppermute | solution.py:17
  187.5 2.7 collective-permute-start.5
  190.9 2.5 multiply_add_fusion
  193.4 2.4 multiply_reduce_fusion.1
  196.1 3.1 fusion.101
  201.1 2.8 fusion.70
  203.9 29.1 %collective-permute-done.4 = f32[4,512,128]{2,1,0:T(8,128)} collective-permute-done((f32[4,512,128]{2,1,0:T(8,128)}, f32[4,512,128]{2,1,0:T(8,128)}, u32[]{:S(2)}, u32[]{:S(2)}) %collective-permute-start.4) | collective-permute-done | bytes 1048608 | tf_op jit(solution)/shard_map/ppermute | solution.py:17
  233.0 24.5 %collective-permute-done.5 = f32[4,512,128]{2,1,0:T(8,128)} collective-permute-done((f32[4,512,128]{2,1,0:T(8,128)}, f32[4,512,128]{2,1,0:T(8,128)}, u32[]{:S(2)}, u32[]{:S(2)}) %collective-permute-start.5) | collective-permute-done | bytes 1048608 | tf_op jit(solution)/shard_map/ppermute | solution.py:17
  257.5 2.0 add_bitcast_fusion
  263.8 105.7 %all-reduce = (f32[128]{0:T(128)}, f32[128]{0:T(128)}) all-reduce(f32[128]{0:T(128)S(1)} %bitcast_reduce_fusion, f32[128]{0:T(128)S(1)} %bitcast_reduce_fusion.1), channel_id=1, replica_groups=mesh['seq'=64,'head'=4] {'seq','head'}, use_global_device_ids=true, to_apply=%region_19.20 | all-reduce | flops 256 | bytes 2048 | tf_op jit(solution)/shard_map/psum | solution.py:213
  369.5 2.5 copy_bitcast_fusion
  (119 shorter events, 26.1 us)
Async XLA Ops:
  0.6 4.1 %copy-start.1 = (bf16[512,512]{1,0:T(8,128)(2,1)S(1)}, bf16[512,512]{1,0:T(8,128)(2,1)}, u32[]{:S(2)}) copy-start(bf16[512,512]{1,0:T(8,128)(2,1)} %param.11) | copy-start | bytes 1572868
  0.6 4.1 %copy-start.14 = (f32[128]{0:T(128)S(1)}, f32[128]{0:T(128)}, u32[]{:S(2)}) copy-start(f32[128]{0:T(128)} %param.15) | copy-start | bytes 1540
  3.7 1.8 copy-start.11
  5.1 7.5 %copy-start.10 = (bf16[512,512]{1,0:T(8,128)(2,1)S(1)}, bf16[512,512]{1,0:T(8,128)(2,1)}, u32[]{:S(2)}) copy-start(bf16[512,512]{1,0:T(8,128)(2,1)} %param.12) | copy-start | bytes 1572868
  5.6 0.8 copy-start.4
  5.6 12.7 %copy-start.5 = (bf16[512,1024]{1,0:T(8,128)(2,1)S(1)}, bf16[512,1024]{1,0:T(8,128)(2,1)}, u32[]{:S(2)}) copy-start(bf16[512,1024]{1,0:T(8,128)(2,1)} %param.10) | copy-start | bytes 3145732
  7.5 19.7 %collective-permute-start = (bf16[512,4,128]{2,0,1:T(8,128)(2,1)}, bf16[512,4,128]{2,0,1:T(8,128)(2,1)}, u32[]{:S(2)}, u32[]{:S(2)}) collective-permute-start(bf16[512,4,128]{2,0,1:T(8,128)(2,1)} %pad_maximum_fusion.2), channel_id=1, source_target_pairs={{0,4},{4,8},{8,12},{12,16},{16,20},{20,24},{24,28},{28,32},{32,36}... | collective-permute-start | bytes 1572872 | tf_op jit(solution)/shard_map/ppermute | solution.py:17
  9.4 40.5 %collective-permute-start.1 = (bf16[512,4,128]{2,0,1:T(8,128)(2,1)}, bf16[512,4,128]{2,0,1:T(8,128)(2,1)}, u32[]{:S(2)}, u32[]{:S(2)}) collective-permute-start(bf16[512,4,128]{2,0,1:T(8,128)(2,1)} %pad_maximum_fusion.2), channel_id=1, source_target_pairs={{0,8},{4,12},{8,16},{12,20},{16,24},{20,28},{24,32},{28,36},{32,40... | collective-permute-start | bytes 1572872 | tf_op jit(solution)/shard_map/ppermute | solution.py:17
  13.7 46.9 %collective-permute-start.2 = (bf16[512,4,128]{0,2,1:T(8,128)(2,1)}, bf16[512,4,128]{0,2,1:T(8,128)(2,1)}, u32[]{:S(2)}, u32[]{:S(2)}) collective-permute-start(bf16[512,4,128]{0,2,1:T(8,128)(2,1)} %bitcast.6), channel_id=1, source_target_pairs={{0,4},{4,8},{8,12},{12,16},{16,20},{20,24},{24,28},{28,32},{32,36}... | collective-permute-start | bytes 1572872 | tf_op jit(solution)/shard_map/ppermute | solution.py:17
  16.8 56.1 %collective-permute-start.3 = (bf16[512,4,128]{0,2,1:T(8,128)(2,1)}, bf16[512,4,128]{0,2,1:T(8,128)(2,1)}, u32[]{:S(2)}, u32[]{:S(2)}) collective-permute-start(bf16[512,4,128]{0,2,1:T(8,128)(2,1)} %bitcast.6), channel_id=1, source_target_pairs={{0,8},{4,12},{8,16},{12,20},{16,24},{20,28},{24,32},{28,36},{32,40... | collective-permute-start | bytes 1572872 | tf_op jit(solution)/shard_map/ppermute | solution.py:17
  19.0 0.9 copy-start.13
  19.9 0.9 copy-start.7
  21.7 0.7 copy-start.15
  83.0 4.2 %slice-start = ((s8[6291456]{0:T(1024)(128)(4,1)}), s8[4194304]{0:T(1024)(128)(4,1)S(1)}, s32[]{:S(2)}) async-start(s8[6291456]{0:T(1024)(128)(4,1)} %bitcast.185), calls=%async_computation | async-start | bytes 8388608 | tf_op jit(solution)/shard_map/while
  83.0 4.9 %slice-start.1 = ((s8[6291456]{0:T(1024)(128)(4,1)}), s8[2097152]{0:T(1024)(128)(4,1)S(1)}, s32[]{:S(2)}) async-start(s8[6291456]{0:T(1024)(128)(4,1)} %bitcast.185), calls=%async_computation.1 | async-start | bytes 4194304 | tf_op jit(solution)/shard_map/while
  107.4 4.2 %slice-start = ((s8[6291456]{0:T(1024)(128)(4,1)}), s8[4194304]{0:T(1024)(128)(4,1)S(1)}, s32[]{:S(2)}) async-start(s8[6291456]{0:T(1024)(128)(4,1)} %bitcast.185), calls=%async_computation | async-start | bytes 8388608 | tf_op jit(solution)/shard_map/while
  107.4 4.9 %slice-start.1 = ((s8[6291456]{0:T(1024)(128)(4,1)}), s8[2097152]{0:T(1024)(128)(4,1)S(1)}, s32[]{:S(2)}) async-start(s8[6291456]{0:T(1024)(128)(4,1)} %bitcast.185), calls=%async_computation.1 | async-start | bytes 4194304 | tf_op jit(solution)/shard_map/while
  131.9 4.2 %slice-start = ((s8[6291456]{0:T(1024)(128)(4,1)}), s8[4194304]{0:T(1024)(128)(4,1)S(1)}, s32[]{:S(2)}) async-start(s8[6291456]{0:T(1024)(128)(4,1)} %bitcast.185), calls=%async_computation | async-start | bytes 8388608 | tf_op jit(solution)/shard_map/while
  131.9 4.9 %slice-start.1 = ((s8[6291456]{0:T(1024)(128)(4,1)}), s8[2097152]{0:T(1024)(128)(4,1)S(1)}, s32[]{:S(2)}) async-start(s8[6291456]{0:T(1024)(128)(4,1)} %bitcast.185), calls=%async_computation.1 | async-start | bytes 4194304 | tf_op jit(solution)/shard_map/while
  156.4 4.2 %slice-start = ((s8[6291456]{0:T(1024)(128)(4,1)}), s8[4194304]{0:T(1024)(128)(4,1)S(1)}, s32[]{:S(2)}) async-start(s8[6291456]{0:T(1024)(128)(4,1)} %bitcast.185), calls=%async_computation | async-start | bytes 8388608 | tf_op jit(solution)/shard_map/while
  156.4 4.9 %slice-start.1 = ((s8[6291456]{0:T(1024)(128)(4,1)}), s8[2097152]{0:T(1024)(128)(4,1)S(1)}, s32[]{:S(2)}) async-start(s8[6291456]{0:T(1024)(128)(4,1)} %bitcast.185), calls=%async_computation.1 | async-start | bytes 4194304 | tf_op jit(solution)/shard_map/while
  173.3 16.8 %copy-start.3 = (f32[4,2,512,128]{3,2,1,0:T(8,128)S(1)}, f32[4,2,512,128]{3,2,1,0:T(8,128)}, u32[]{:S(2)}) copy-start(f32[4,2,512,128]{3,2,1,0:T(8,128)} %get-tuple-element.54) | copy-start | bytes 6291460
  176.5 56.5 %collective-permute-start.4 = (f32[4,512,128]{2,1,0:T(8,128)}, f32[4,512,128]{2,1,0:T(8,128)}, u32[]{:S(2)}, u32[]{:S(2)}) collective-permute-start(f32[4,512,128]{2,1,0:T(8,128)} %get-tuple-element.213), channel_id=1, source_target_pairs={{0,252},{4,0},{8,4},{12,8},{16,12},{20,16},{24,20},{28,24},{32,28}... | collective-permute-start | bytes 3145736 | tf_op jit(solution)/shard_map/ppermute | solution.py:17
  187.5 70.0 %collective-permute-start.5 = (f32[4,512,128]{2,1,0:T(8,128)}, f32[4,512,128]{2,1,0:T(8,128)}, u32[]{:S(2)}, u32[]{:S(2)}) collective-permute-start(f32[4,512,128]{2,1,0:T(8,128)} %get-tuple-element.214), channel_id=1, source_target_pairs={{0,248},{4,252},{8,0},{12,4},{16,8},{20,12},{24,16},{28,20},{32,24... | collective-permute-start | bytes 3145736 | tf_op jit(solution)/shard_map/ppermute | solution.py:17
  199.2 0.9 copy-start.8
  199.2 170.3 %collective-permute-start.6 = (f32[4,512,128]{2,1,0:T(8,128)}, f32[4,512,128]{2,1,0:T(8,128)S(1)}, u32[]{:S(2)}, u32[]{:S(2)}) collective-permute-start(f32[4,512,128]{2,1,0:T(8,128)} %get-tuple-element.211), channel_id=1, source_target_pairs={{0,252},{4,0},{8,4},{12,8},{16,12},{20,16},{24,20},{28,24},{32,28}... | collective-permute-start | bytes 3145736 | tf_op jit(solution)/shard_map/ppermute | solution.py:17
  199.2 1.7 copy-start
  199.2 1.9 copy-start.6
  199.2 170.3 %collective-permute-start.7 = (f32[4,512,128]{2,1,0:T(8,128)}, f32[4,512,128]{2,1,0:T(8,128)}, u32[]{:S(2)}, u32[]{:S(2)}) collective-permute-start(f32[4,512,128]{2,1,0:T(8,128)} %get-tuple-element.212), channel_id=1, source_target_pairs={{0,248},{4,252},{8,0},{12,4},{16,8},{20,12},{24,16},{28,20},{32,24... | collective-permute-start | bytes 3145736 | tf_op jit(solution)/shard_map/ppermute | solution.py:17
  259.5 1.0 copy-start.2
  260.0 1.2 copy-start.12
  260.6 1.4 copy-start.9
where the time goes:
time: 373 us; the launch traced here: 372 us
  blocking collectives  106 us (28%)
  waiting for transfers between devices  96.4 us (26%)
  matrix products  85.9 us (23%)
  other arithmetic  38.2 us (10%)
  starting transfers between devices  23.5 us (6%)
  local copies, waits for them, and re-layouts  21 us (6%)
    psum x1, blocking collectives, shards(): lax.psum((query_gain_part, key_gain_part), ('seq', 'head'))  106 us
    ppermute x8, waiting for transfers between devices, from_behind(): lax.ppermute(shard, axis, [(i, (i + by) % peers) for i in range(peers)])  96.4 us
    sub x4, matrix products, head_forward(): exponent = jnp.exp(scores - row_max)  24.6 us
    ppermute x8, starting transfers between devices, from_behind(): lax.ppermute(shard, axis, [(i, (i + by) % peers) for i in range(peers)])  23.5 us
    dot_general x4, matrix products, per_head(): jnp.einsum('grk,grd->kd', soft_half, grad_group, preferred_element_type=j...  21.6 us
    dot_general x4, matrix products, head_forward(): jnp.einsum('grd,kd->grk', grad_group, value_block, preferred_element_type...  16.9 us
    dot_general x4, matrix products, per_head(): jnp.einsum('grk,grd->kd', grad_scores, query_group, preferred_element_typ...  11.6 us
    dot_general x4, matrix products, per_head(): jnp.einsum('grk,kd->grd', grad_scores, key_block, preferred_element_type=...  11.2 us
  transfers between devices with their start and end apart: 8, of which 5 were waited for; matrix products, arithmetic and copies ran while one was open for 8% of the time, Pallas kernels for 0%

commit v1 on v0

v1 whole, which is shorter than its diff:
```python
import functools
import math

import jax
import jax.numpy as jnp
from jax import lax
from jax.experimental import pallas as pl
from jax.experimental.pallas import tpu as pltpu
from jax.sharding import PartitionSpec as P

SLABS = 4
ROWS = 512
TILE = 256
SPAN = 1280
KEYS = 1536
DIM = 128
HEADS = 4

score_scale = 168.0 ** (-0.5)
exp2_scale = score_scale * math.log2(math.e)
norm_eps = 1e-06
masked_score = -1e30
f32 = jnp.float32
bf16 = jnp.bfloat16
MESH = pl.DeviceIdType.MESH


def half_turn(x):
    return pltpu.roll(x, DIM // 2, 1)


def unit_rows(raw):
    x = raw.astype(f32)
    inverse = lax.rsqrt(jnp.mean(x * x, axis=-1, keepdims=True) + norm_eps)
    return x * inverse, inverse


def fold_rows(x):
    return jnp.sum(x.reshape(x.shape[0] // 8, 8, DIM), axis=0)


def cos_sin(angle, cos_lane):
    turns = jnp.floor(angle * (2.0 / math.pi) + 0.5)
    rest = angle - turns * 1.5703125
    rest = rest - turns * 4.837512969970703e-4
    rest = rest - turns * 7.549789954891882e-8
    square = rest * rest
    sine = rest + rest * square * (
        -1.6666654611e-1 + square * (8.3321608736e-3 - square * 1.9515295891e-4)
    )
    cosine = 1.0 - 0.5 * square + square * square * (
        4.166664568298827e-2 + square * (-1.388731625493765e-3 + square * 2.443315711809948e-5)
    )
    quarter = turns + jnp.where(cos_lane, 1.0, 0.0)
    quarter = quarter - 4.0 * jnp.floor(quarter * 0.25)
    odd = (quarter == 1.0) | (quarter == 3.0)
    value = jnp.where(odd, cosine, sine)
    return jnp.where(quarter >= 2.0, -value, value)


def kernel(
    shards,
    heads,
    q_hbm,
    k_hbm,
    v_hbm,
    do_hbm,
    query_gain,
    key_gain,
    inverse_freq,
    doc_starts,
    windows,
    dq_hbm,
    dk_hbm,
    dv_hbm,
    gain_out,
    kcat,
    vcat,
    q_all,
    do_all,
    cos_table,
    sin_table,
    khat,
    kunit,
    qhat,
    qunit,
    qinv,
    dos,
    scores,
    soft_grad,
    acc_k,
    acc_v,
    far_send,
    far_in,
    near_send,
    near_in,
    dq_all,
    dk_all,
    dv_all,
    gain_acc,
    sum_send,
    sum_in,
    local_sem,
    out_sem,
    fwd_send,
    fwd_recv,
    relay_send,
    relay_recv,
    far_ssem,
    far_rsem,
    near_ssem,
    near_rsem,
    sum_ssem,
    sum_rsem,
):
    total = shards * ROWS
    length = total // SLABS
    me = lax.axis_index("seq")
    my_head = lax.axis_index("head")
    ahead = lax.rem(me + 1, shards)
    behind = lax.rem(me + shards - 1, shards)
    low_size = min(8, shards)
    high_size = shards // low_size
    my_low = lax.rem(me, low_size)
    my_high = me // low_size
    stages = [
        (heads, my_head, lambda n: (me, n)),
        (low_size, my_low, lambda n: (my_high * low_size + n, my_head)),
        (high_size, my_high, lambda n: (n * low_size + my_low, my_head)),
    ]

    barrier = pltpu.get_barrier_semaphore()
    pl.semaphore_signal(barrier, inc=1, device_id=(ahead, my_head), device_id_type=MESH)
    pl.semaphore_signal(barrier, inc=1, device_id=(behind, my_head), device_id_type=MESH)
    greeted = 2
    for size, mine, place in stages:
        for k in range(1, size):
            pl.semaphore_signal(
                barrier,
                inc=1,
                device_id=place(lax.rem(mine + k, size)),
                device_id_type=MESH,
            )
            greeted += 1
    pl.semaphore_wait(barrier, greeted)

    def columns(j, width=DIM):
        return pl.ds(pl.multiple_of(j * width, width), width)

    def own_copies(j):
        return [
            pltpu.make_async_remote_copy(
                src_ref=src.at[:, columns(j)],
                dst_ref=dst.at[j, pl.ds(ROWS, ROWS), :],
                send_sem=fwd_send.at[j, n],
                recv_sem=fwd_recv.at[j, n],
                device_id=(ahead, my_head),
                device_id_type=MESH,
            )
            for n, (src, dst) in enumerate(((k_hbm, kcat), (v_hbm, vcat)))
        ]

    def relay_copies(j):
        return [
            pltpu.make_async_remote_copy(
                src_ref=buf.at[j, pl.ds(ROWS, ROWS), :],
                dst_ref=buf.at[j, pl.ds(0, ROWS), :],
                send_sem=relay_send.at[j, n],
                recv_sem=relay_recv.at[j, n],
                device_id=(ahead, my_head),
                device_id_type=MESH,
            )
            for n, buf in enumerate((kcat, vcat))
        ]

    def back_copies(j, src, dst, ssem, rsem):
        return [
            pltpu.make_async_remote_copy(
                src_ref=src.at[j, n],
                dst_ref=dst.at[j, n],
                send_sem=ssem.at[j, n],
                recv_sem=rsem.at[j, n],
                device_id=(behind, my_head),
                device_id_type=MESH,
            )
            for n in range(2)
        ]

    def far_copies(j):
        return back_copies(j, far_send, far_in, far_ssem, far_rsem)

    def near_copies(j):
        return back_copies(j, near_send, near_in, near_ssem, near_rsem)

    def start_own(j):
        for copy in own_copies(j):
            copy.start()

    def relay(j):
        for arrived, onward in zip(own_copies(j), relay_copies(j)):
            arrived.wait_recv()
            onward.start()

    start_own(0)
    start_own(1)
    local = []
    for j in range(HEADS):
        local.append((k_hbm.at[:, columns(j)], kcat.at[j, pl.ds(2 * ROWS, ROWS), :]))
        local.append((v_hbm.at[:, columns(j)], vcat.at[j, pl.ds(2 * ROWS, ROWS), :]))
    local.append((q_hbm, q_all))
    local.append((do_hbm, do_all))
    local = [
        pltpu.make_async_copy(src, dst, local_sem.at[n]) for n, (src, dst) in enumerate(local)
    ]
    for copy in local:
        copy.start()

    def block_info(block):
        shard = lax.rem(me + shards - 2 + block, shards)
        placed = lax.rem(shard * ROWS + total - length // 2, total)
        slab = placed // length
        return slab, placed - slab * length

    def rope_position(in_slab, slab):
        begin = jnp.zeros_like(in_slab)
        for n in range(doc_starts.shape[1]):
            start = doc_starts[slab, n]
            begin = jnp.where(in_slab >= start, jnp.maximum(begin, start), begin)
        return in_slab - begin

    lane = lax.broadcasted_iota(jnp.int32, (TILE, DIM), 1)
    cos_lane = lane < DIM // 2

    def table_step(n, carry):
        block = n // (ROWS // TILE)
        slab, first = block_info(block)
        offset = lax.rem(n, ROWS // TILE) * TILE
        in_slab = first + offset + lax.broadcasted_iota(jnp.int32, (TILE, DIM), 0)
        position = rope_position(in_slab, slab).astype(f32)
        both = cos_sin(position * inverse_freq[...], cos_lane)
        other = half_turn(both)
        here = pl.ds(pl.multiple_of(n * TILE, TILE), TILE)
        cos_table[here, :] = jnp.where(cos_lane, both, other)
        sin_table[here, :] = jnp.where(cos_lane, -other, both)
        return carry

    lax.fori_loop(0, KEYS // TILE, table_step, 0)
    gain_acc[...] = jnp.zeros_like(gain_acc)

    relay(0)
    start_own(2)
    for copy in local:
        copy.wait()

    slab, first = block_info(2)
    window = windows[slab]

    def key_norm(j, start, count):
        def step(n, carry):
            here = pl.ds(pl.multiple_of(start + n * TILE, TILE), TILE)
            unit, _ = unit_rows(kcat[j, here, :])
            scaled = unit * key_gain[...]
            khat[here, :] = (
                scaled * cos_table[here, :] + half_turn(scaled) * sin_table[here, :]
            ).astype(bf16)
            kunit[here, :] = unit
            return carry

        lax.fori_loop(0, count // TILE, step, 0)

    nt = (((1,), (1,)), ((), ()))
    nn = (((1,), (0,)), ((), ()))
    tn = (((0,), (0,)), ((), ()))

    def attend(j, i):
        base = i * TILE
        rows = pl.ds(pl.multiple_of(base, TILE), TILE)
        mine = pl.ds(pl.multiple_of(base + 2 * ROWS, TILE), TILE)
        for g in range(2):
            head_columns = pl.ds(pl.multiple_of((2 * j + g) * DIM, DIM), DIM)
            part = pl.ds(g * TILE, TILE)
            unit, inverse = unit_rows(q_all[rows, head_columns])
            scaled = unit * query_gain[...]
            qhat[part, :] = (
                scaled * cos_table[mine, :] + half_turn(scaled) * sin_table[mine, :]
            ).astype(bf16)
            qunit[part, :] = unit
            qinv[part, :] = jnp.broadcast_to(inverse, (TILE, DIM))
            dos[part, :] = do_all[rows, head_columns]
        q = qhat[...]
        out_grad = dos[...]

        row = lax.rem(lax.broadcasted_iota(jnp.int32, (1, 2 * TILE), 1), TILE)
        in_slab = first + base + row
        reach = jnp.minimum(rope_position(in_slab, slab), window - 1)
        lowest = 2 * ROWS + row - reach
        key_row = lax.broadcasted_iota(jnp.int32, (TILE, 2 * TILE), 0)

        row_max = jnp.full((1, 2 * TILE), masked_score, f32)
        for t in range(SPAN // TILE):
            keys = khat[pl.ds(pl.multiple_of(base + t * TILE, TILE), TILE), :]
            tile = lax.dot_general(keys, q, nt, preferred_element_type=f32)
            visible = key_row >= lowest - t * TILE
            if t == SPAN // TILE - 1:
                visible = visible & (key_row <= row)
            tile = jnp.where(visible, tile, masked_score)
            scores[pl.ds(t * TILE, TILE), :] = tile
            row_max = jnp.maximum(row_max, jnp.max(tile, axis=0, keepdims=True))
        shift = row_max * exp2_scale
        row_sum = jnp.zeros((1, 2 * TILE), f32)
        delta = jnp.zeros((1, 2 * TILE), f32)
        for t in range(SPAN // TILE):
            here = pl.ds(t * TILE, TILE)
            values = vcat[j, pl.ds(pl.multiple_of(base + t * TILE, TILE), TILE), :]
            gradient = lax.dot_general(values, out_grad, nt, preferred_element_type=f32)
            exponent = jnp.exp2(scores[here, :] * exp2_scale - shift)
            row_sum += jnp.sum(exponent, axis=0, keepdims=True)
            delta += jnp.sum(exponent * gradient, axis=0, keepdims=True)
            scores[here, :] = exponent
            soft_grad[here, :] = gradient
        inverse_sum = 1.0 / row_sum
        delta = delta * inverse_sum
        query_grad = jnp.zeros((2 * TILE, DIM), f32)
        for t in range(SPAN // TILE):
            here = pl.ds(t * TILE, TILE)
            there = pl.ds(pl.multiple_of(base + t * TILE, TILE), TILE)
            softmax = scores[here, :] * inverse_sum
            grad_scores = (softmax * (soft_grad[here, :] - delta)).astype(bf16)
            acc_v[j, there, :] += lax.dot_general(
                softmax.astype(bf16), out_grad, nn, preferred_element_type=f32
            )
            acc_k[j, there, :] += lax.dot_general(
                grad_scores, q, nn, preferred_element_type=f32
            )
            query_grad += lax.dot_general(
                grad_scores, khat[there, :], tn, preferred_element_type=f32
            )
        for g in range(2):
            head_columns = pl.ds(pl.multiple_of((2 * j + g) * DIM, DIM), DIM)
            part = pl.ds(g * TILE, TILE)
            grad = query_grad[g * TILE : (g + 1) * TILE] * score_scale
            turned = grad * cos_table[mine, :] - half_turn(grad) * sin_table[mine, :]
            unit = qunit[part, :]
            gain_acc[0] += fold_rows(turned * unit)
            weighted = turned * query_gain[...]
            mean = jnp.mean(weighted * unit, axis=-1, keepdims=True)
            dq_all[rows, head_columns] = (qinv[part, :] * (weighted - unit * mean)).astype(bf16)

    def dq_copy(j):
        return pltpu.make_async_copy(
            dq_all.at[:, columns(j, 2 * DIM)], dq_hbm.at[:, columns(j, 2 * DIM)], out_sem.at[j, 0]
        )

    def dk_copy(j):
        return pltpu.make_async_copy(
            dk_all.at[:, columns(j)], dk_hbm.at[:, columns(j)], out_sem.at[j, 1]
        )

    def dv_copy(j):
        return pltpu.make_async_copy(
            dv_all.at[:, columns(j)], dv_hbm.at[:, columns(j)], out_sem.at[j, 2]
        )

    def hand_on(j):
        for n, (copy, onward, acc) in enumerate(
            zip(far_copies(j), near_copies(j), (acc_k, acc_v))
        ):
            copy.wait_recv()
            near_send[j, n] = (
                far_in[j, n].astype(f32) + acc[j, pl.ds(ROWS, ROWS), :]
            ).astype(bf16)
            onward.start()

    def finish(j):
        key_copy, value_copy = near_copies(j)
        key_copy.wait_recv()

        def key_step(n, carry):
            rows = pl.ds(pl.multiple_of(n * TILE, TILE), TILE)
            mine = pl.ds(pl.multiple_of(2 * ROWS + n * TILE, TILE), TILE)
            grad = (near_in[j, 0, rows, :].astype(f32) + acc_k[j, mine, :]) * score_scale
            turned = grad * cos_table[mine, :] - half_turn(grad) * sin_table[mine, :]
            unit, inverse = unit_rows(kcat[j, mine, :])
            weighted = turned * key_gain[...]
            mean = jnp.mean(weighted * unit, axis=-1, keepdims=True)
            dk_all[rows, columns(j)] = (inverse * (weighted - unit * mean)).astype(bf16)
            return carry

        lax.fori_loop(0, ROWS // TILE, key_step, 0)
        dk_copy(j).start()
        value_copy.wait_recv()

        def value_step(n, carry):
            rows = pl.ds(pl.multiple_of(n * TILE, TILE), TILE)
            mine = pl.ds(pl.multiple_of(2 * ROWS + n * TILE, TILE), TILE)
            dv_all[rows, columns(j)] = (
                near_in[j, 1, rows, :].astype(f32) + acc_v[j, mine, :]
            ).astype(bf16)
            return carry

        lax.fori_loop(0, ROWS // TILE, value_step, 0)
        dv_copy(j).start()

    def head_step(j, carry):
        key_norm(j, ROWS, 2 * ROWS)
        acc_k[j] = jnp.zeros((KEYS, DIM), f32)
        acc_v[j] = jnp.zeros((KEYS, DIM), f32)

        @pl.when(j < HEADS - 1)
        def _():
            relay(j + 1)

        @pl.when(j < HEADS - 3)
        def _():
            start_own(j + 3)

        for copy in relay_copies(j):
            copy.wait_recv()
        key_norm(j, 0, ROWS)

        def row_step(i, inner):
            attend(j, i)
            return inner

        lax.fori_loop(0, ROWS // TILE, row_step, 0)
        far_send[j, 0] = acc_k[j, pl.ds(0, ROWS), :].astype(bf16)
        far_send[j, 1] = acc_v[j, pl.ds(0, ROWS), :].astype(bf16)
        for copy in far_copies(j):
            copy.start()
        dq_copy(j).start()

        def gain_step(n, inner):
            here = pl.ds(pl.multiple_of(n * TILE, TILE), TILE)
            grad = acc_k[j, here, :] * score_scale
            turned = grad * cos_table[here, :] - half_turn(grad) * sin_table[here, :]
            gain_acc[1] += fold_rows(turned * kunit[here, :])
            return inner

        lax.fori_loop(0, KEYS // TILE, gain_step, 0)

        @pl.when(j >= 1)
        def _():
            hand_on(j - 1)

        @pl.when(j >= 2)
        def _():
            finish(j - 2)

        return carry

    lax.fori_loop(0, HEADS, head_step, 0)

    def sum_copy(n, k):
        size, mine, place = stages[n]
        return pltpu.make_async_remote_copy(
            src_ref=sum_send.at[n],
            dst_ref=sum_in.at[n, mine],
            send_sem=sum_ssem.at[n, k],
            recv_sem=sum_rsem.at[n, mine],
            device_id=place(lax.rem(mine + k, size)),
            device_id_type=MESH,
        )

    def sum_arrival(n, k):
        size, mine, place = stages[n]
        source = lax.rem(mine + size - k, size)
        return pltpu.make_async_remote_copy(
            src_ref=sum_send.at[n],
            dst_ref=sum_in.at[n, source],
            send_sem=sum_ssem.at[n, k],
            recv_sem=sum_rsem.at[n, source],
            device_id=place(source),
            device_id_type=MESH,
        )

    def start_sum(n, value):
        size, mine, place = stages[n]
        sum_send[n] = value
        sum_in[n, mine] = value
        for k in range(1, size):
            sum_copy(n, k).start()

    def end_sum(n):
        size, mine, place = stages[n]
        for k in range(1, size):
            sum_arrival(n, k).wait_recv()
        value = sum_in[n, 0]
        for k in range(1, size):
            value = value + sum_in[n, k]
        return value

    spread = jnp.where(
        lax.broadcasted_iota(jnp.int32, (8, DIM), 0) == 0,
        jnp.sum(gain_acc[0], axis=0, keepdims=True),
        jnp.sum(gain_acc[1], axis=0, keepdims=True),
    )
    start_sum(0, spread)
    hand_on(HEADS - 1)
    start_sum(1, end_sum(0))
    finish(HEADS - 2)
    start_sum(2, end_sum(1))
    gain_out[...] = end_sum(2)
    finish(HEADS - 1)

    for n, (size, mine, place) in enumerate(stages):
        for k in range(1, size):
            sum_copy(n, k).wait_send()

    def drain(j, carry):
        for copies in (own_copies(j), relay_copies(j), far_copies(j), near_copies(j)):
            for copy in copies:
                copy.wait_send()
        dq_copy(j).wait()
        dk_copy(j).wait()
        dv_copy(j).wait()
        return carry

    lax.fori_loop(0, HEADS, drain, 0)


def solution(mesh):
    shards, heads = mesh.shape["seq"], mesh.shape["head"]
    most = max(heads, 8, shards // 8)

    def step(q, k, v, out_grad, query_gain, key_gain, doc_starts, windows):
        spacing = jnp.arange(DIM // 2, dtype=f32) * (2.0 / DIM)
        inverse_freq = 10000.0 ** (-spacing)
        inverse_freq = jnp.concatenate([inverse_freq, inverse_freq])[None]
        hbm = pl.BlockSpec(memory_space=pl.ANY)
        vmem = pl.BlockSpec(memory_space=pltpu.VMEM)
        smem = pl.BlockSpec(memory_space=pltpu.SMEM)
        dq, dk, dv, gains = pl.pallas_call(
            functools.partial(kernel, shards, heads),
            out_shape=(
                jax.ShapeDtypeStruct(q.shape, bf16),
                jax.ShapeDtypeStruct(k.shape, bf16),
                jax.ShapeDtypeStruct(v.shape, bf16),
                jax.ShapeDtypeStruct((8, DIM), f32),
            ),
            in_specs=[hbm] * 4 + [vmem] * 3 + [smem] * 2,
            out_specs=(hbm, hbm, hbm, vmem),
            scratch_shapes=[
                pltpu.VMEM((HEADS, KEYS, DIM), bf16),
                pltpu.VMEM((HEADS, KEYS, DIM), bf16),
                pltpu.VMEM((ROWS, 2 * HEADS * DIM), bf16),
                pltpu.VMEM((ROWS, 2 * HEADS * DIM), bf16),
                pltpu.VMEM((KEYS, DIM), f32),
                pltpu.VMEM((KEYS, DIM), f32),
                pltpu.VMEM((KEYS, DIM), bf16),
                pltpu.VMEM((KEYS, DIM), f32),
                pltpu.VMEM((2 * TILE, DIM), bf16),
                pltpu.VMEM((2 * TILE, DIM), f32),
                pltpu.VMEM((2 * TILE, DIM), f32),
                pltpu.VMEM((2 * TILE, DIM), bf16),
                pltpu.VMEM((SPAN, 2 * TILE), f32),
                pltpu.VMEM((SPAN, 2 * TILE), f32),
                pltpu.VMEM((HEADS, KEYS, DIM), f32),
                pltpu.VMEM((HEADS, KEYS, DIM), f32),
                pltpu.VMEM((HEADS, 2, ROWS, DIM), bf16),
                pltpu.VMEM((HEADS, 2, ROWS, DIM), bf16),
                pltpu.VMEM((HEADS, 2, ROWS, DIM), bf16),
                pltpu.VMEM((HEADS, 2, ROWS, DIM), bf16),
                pltpu.VMEM((ROWS, 2 * HEADS * DIM), bf16),
                pltpu.VMEM((ROWS, HEADS * DIM), bf16),
                pltpu.VMEM((ROWS, HEADS * DIM), bf16),
                pltpu.VMEM((2, 8, DIM), f32),
                pltpu.VMEM((3, 8, DIM), f32),
                pltpu.VMEM((3, most, 8, DIM), f32),
                pltpu.SemaphoreType.DMA((2 * HEADS + 2,)),
                pltpu.SemaphoreType.DMA((HEADS, 3)),
            ]
            + [pltpu.SemaphoreType.DMA((HEADS, 2)) for _ in range(8)]
            + [pltpu.SemaphoreType.DMA((3, most)) for _ in range(2)],
            compiler_params=pltpu.CompilerParams(
                collective_id=0, has_side_effects=True, vmem_limit_bytes=60 * 1024 * 1024
            ),
        )(
            q,
            k,
            v,
            out_grad,
            query_gain[None],
            key_gain[None],
            inverse_freq,
            doc_starts,
            windows,
        )
        return dq, dk, dv, gains[0], gains[1]

    split = P("seq", "head")
    return jax.shard_map(
        step,
        mesh=mesh,
        in_specs=(split,) * 4 + (P(),) * 4,
        out_specs=(split, split, split, P(), P()),
        check_vma=False,
    )
```

time: 373 us -> 105 us (0.28)
  blocking collectives: 106 us -> 0 us
  Pallas kernels: 0 us -> 98 us
  waiting for transfers between devices: 96.4 us -> 0 us
  matrix products: 85.9 us -> 0 us
  other arithmetic: 38.2 us -> 0.6 us
  starting transfers between devices: 23.5 us -> 0 us
  local copies, waits for them, and re-layouts: 21 us -> 5.62 us
    psum x1 -> x0, blocking collectives: 106 us -> none  [shards(): lax.psum((query_gain_part, key_gain_part), ('seq', 'head'))]
    pallas_call x0 -> x1, Pallas kernels: none -> 98 us  [step(): pl.pallas_call(functools.partial(kernel, shards, heads), out_shape=(jax.S...]
    ppermute x8 -> x0, waiting for transfers between devices: 96.4 us -> none  [from_behind(): lax.ppermute(shard, axis, [(i, (i + by) % peers) for i in range(peers)])]
    dot_general x16 -> x0, matrix products: 61.3 us -> none  [the longest x4 21.6 us: per_head(): jnp.einsum('grk,grd->kd', soft_half, grad_group, preferred_element_type=j...]
    sub x4 -> x0, matrix products: 24.6 us -> none  [head_forward(): exponent = jnp.exp(scores - row_max)]
    ppermute x8 -> x0, starting transfers between devices: 23.5 us -> none  [from_behind(): lax.ppermute(shard, axis, [(i, (i + by) % peers) for i in range(peers)])]
    transpose x4 -> x0, other arithmetic: 9.02 us -> none  [the longest x1 2.86 us: shards(): keys_heads = jnp.transpose(jnp.concatenate(key_sequence_list, 0), (1, 0, 2))]
    reduce_sum x12 -> x0, other arithmetic: 8.61 us -> none  [the longest x4 4.03 us: norm_backward(): gain_grad = jnp.sum(grad_scaled * unit_rows, axis=(0, 1))]
  transfers between devices with their start and end apart: 8 -> 0, of which waited for: 5 -> 0; matrix products, arithmetic and copies ran while one was open for 8% -> 0% of each run, Pallas kernels for 0% -> 0%
where the time goes in v1:
time: 105 us
  Pallas kernels  98 us (93%)
  local copies, waits for them, and re-layouts  5.62 us (5%)
    pallas_call x1, Pallas kernels, step(): pl.pallas_call(functools.partial(kernel, shards, heads), out_shape=(jax.S...  98 us
    unnamed x7, local copies, waits for them, and re-layouts  4.35 us

profile of v1, /device:TPU:2, one launch (start us, length us, event | category | flops | bytes accessed | tf_op | source)
XLA Modules:
  0.0 104.9 jit_solution(2712650688412379285)
XLA Ops:
  0.6 0.6 maximum_bitcast_fusion.inverse_freq
  1.2 98.0 %shard_map.119 = (bf16[512,1024]{1,0:T(8,128)(2,1)}, bf16[512,512]{1,0:T(8,128)(2,1)}, bf16[512,512]{1,0:T(8,128)(2,1)}, f32[8,128]{1,0:T(8,128)}) custom-call(bf16[512,1024]{1,0:T(8,128)(2,1)} %q_hbm.1, bf16[512,512]{1,0:T(8,128)(2,1)} %k_hbm.1, bf16[512,512]{1,0:T(8,128)(2,1)} %v_hbm.1, bf16[512,1024]{1,0:T(8,128)(2,1)} %do_hbm.1, f32[1,128]{1,0:T(1,128)} %bitcast.8, ...), custom_call_target="tpu_custom_call" | custom-call | tf_op jit(solution)/shard_map/pallas_call | solution.py:532
  99.3 1.3 %slice_bitcast_fusion = (f32[128]{0:T(128)}, f32[128]{0:T(128)}) fusion(f32[8,128]{1,0:T(8,128)} %get-tuple-element.12), kind=kLoop, calls=%fused_computation.1 | loop fusion | bytes 2048 | tf_op jit(solution)/shard_map/squeeze | solution.py:588
  100.6 0.0 copy-start.1
  100.6 2.3 %copy.16 = bf16[512,1024]{1,0:T(8,128)(2,1)} copy(bf16[512,1024]{1,0:T(8,128)(2,1)} %get-tuple-element.20) | data formatting | bytes 2097152
  102.9 0.0 copy-done.1
  102.9 0.0 copy-start
  102.9 0.8 copy.17
  103.7 0.4 copy-done
  104.1 0.8 copy.18
  (1 shorter events, 0.0 us)
Async XLA Ops:
  100.6 2.3 %copy-start.1 = (bf16[512,512]{1,0:T(8,128)(2,1)S(1)}, bf16[512,512]{1,0:T(8,128)(2,1)}, u32[]{:S(2)}) copy-start(bf16[512,512]{1,0:T(8,128)(2,1)} %get-tuple-element.21) | copy-start | bytes 1572868
  102.9 1.2 %copy-start = (bf16[512,512]{1,0:T(8,128)(2,1)S(1)}, bf16[512,512]{1,0:T(8,128)(2,1)}, u32[]{:S(2)}) copy-start(bf16[512,512]{1,0:T(8,128)(2,1)} %get-tuple-element.22) | copy-start | bytes 1572868

commit v2 on v1

--- a/solution.py
+++ b/solution.py
@@ -70,10 +70,11 @@
     inverse_freq,
     doc_starts,
     windows,
-    dq_hbm,
-    dk_hbm,
-    dv_hbm,
-    gain_out,
+    dq_all,
+    dk_all,
+    dv_all,
+    query_gain_out,
+    key_gain_out,
     kcat,
     vcat,
     q_all,
@@ -94,14 +95,10 @@
     far_in,
     near_send,
     near_in,
-    dq_all,
-    dk_all,
-    dv_all,
     gain_acc,
     sum_send,
     sum_in,
     local_sem,
-    out_sem,
     fwd_send,
     fwd_recv,
     relay_send,
@@ -147,7 +144,7 @@
     def columns(j, width=DIM):
         return pl.ds(pl.multiple_of(j * width, width), width)
 
-    def own_copies(j):
+    def own_copies(j, which=(0, 1)):
         return [
             pltpu.make_async_remote_copy(
                 src_ref=src.at[:, columns(j)],
@@ -158,9 +155,10 @@
                 device_id_type=MESH,
             )
             for n, (src, dst) in enumerate(((k_hbm, kcat), (v_hbm, vcat)))
+            if n in which
         ]
 
-    def relay_copies(j):
+    def relay_copies(j, which=(0, 1)):
         return [
             pltpu.make_async_remote_copy(
                 src_ref=buf.at[j, pl.ds(ROWS, ROWS), :],
@@ -171,6 +169,7 @@
                 device_id_type=MESH,
             )
             for n, buf in enumerate((kcat, vcat))
+            if n in which
         ]
 
     def back_copies(j, src, dst, ssem, rsem):
@@ -192,17 +191,16 @@
     def near_copies(j):
         return back_copies(j, near_send, near_in, near_ssem, near_rsem)
 
-    def start_own(j):
-        for copy in own_copies(j):
-            copy.start()
-
-    def relay(j):
-        for arrived, onward in zip(own_copies(j), relay_copies(j)):
-            arrived.wait_recv()
-            onward.start()
-
-    start_own(0)
-    start_own(1)
+    def start_own(j, n):
+        own_copies(j, (n,))[0].start()
+
+    def relay(j, n):
+        own_copies(j, (n,))[0].wait_recv()
+        relay_copies(j, (n,))[0].start()
+
+    start_own(0, 0)
+    start_own(0, 1)
+    start_own(1, 0)
     local = []
     for j in range(HEADS):
         local.append((k_hbm.at[:, columns(j)], kcat.at[j, pl.ds(2 * ROWS, ROWS), :]))
@@ -247,10 +245,13 @@
     lax.fori_loop(0, KEYS // TILE, table_step, 0)
     gain_acc[...] = jnp.zeros_like(gain_acc)
 
-    relay(0)
-    start_own(2)
     for copy in local:
         copy.wait()
+    relay(0, 0)
+    relay(0, 1)
+    start_own(1, 1)
+    start_own(2, 0)
+    relay(1, 0)
 
     slab, first = block_info(2)
     window = windows[slab]
@@ -287,79 +288,94 @@
             qunit[part, :] = unit
             qinv[part, :] = jnp.broadcast_to(inverse, (TILE, DIM))
             dos[part, :] = do_all[rows, head_columns]
-        q = qhat[...]
-        out_grad = dos[...]
-
-        row = lax.rem(lax.broadcasted_iota(jnp.int32, (1, 2 * TILE), 1), TILE)
+        row = lax.broadcasted_iota(jnp.int32, (1, TILE), 1)
         in_slab = first + base + row
         reach = jnp.minimum(rope_position(in_slab, slab), window - 1)
         lowest = 2 * ROWS + row - reach
-        key_row = lax.broadcasted_iota(jnp.int32, (TILE, 2 * TILE), 0)
-
-        row_max = jnp.full((1, 2 * TILE), masked_score, f32)
-        for t in range(SPAN // TILE):
-            keys = khat[pl.ds(pl.multiple_of(base + t * TILE, TILE), TILE), :]
-            tile = lax.dot_general(keys, q, nt, preferred_element_type=f32)
+        key_row = lax.broadcasted_iota(jnp.int32, (TILE, TILE), 0)
+        q = [qhat[pl.ds(g * TILE, TILE), :] for g in range(2)]
+        out_grad = [dos[pl.ds(g * TILE, TILE), :] for g in range(2)]
+        row_max = [jnp.full((1, TILE), masked_score, f32)] * 2
+        row_sum = [jnp.zeros((1, TILE), f32)] * 2
+        delta = [jnp.zeros((1, TILE), f32)] * 2
+        query_grad = [jnp.zeros((DIM, TILE), f32)] * 2
+        tiles = SPAN // TILE
+
+        def there(t):
+            return pl.ds(pl.multiple_of(base + t * TILE, TILE), TILE)
+
+        def here(t):
+            return pl.ds(t * TILE, TILE)
+
+        def score_tile(g, t):
+            tile = lax.dot_general(khat[there(t), :], q[g], nt, preferred_element_type=f32)
             visible = key_row >= lowest - t * TILE
-            if t == SPAN // TILE - 1:
+            if t == tiles - 1:
                 visible = visible & (key_row <= row)
             tile = jnp.where(visible, tile, masked_score)
-            scores[pl.ds(t * TILE, TILE), :] = tile
-            row_max = jnp.maximum(row_max, jnp.max(tile, axis=0, keepdims=True))
-        shift = row_max * exp2_scale
-        row_sum = jnp.zeros((1, 2 * TILE), f32)
-        delta = jnp.zeros((1, 2 * TILE), f32)
-        for t in range(SPAN // TILE):
-            here = pl.ds(t * TILE, TILE)
-            values = vcat[j, pl.ds(pl.multiple_of(base + t * TILE, TILE), TILE), :]
-            gradient = lax.dot_general(values, out_grad, nt, preferred_element_type=f32)
-            exponent = jnp.exp2(scores[here, :] * exp2_scale - shift)
-            row_sum += jnp.sum(exponent, axis=0, keepdims=True)
-            delta += jnp.sum(exponent * gradient, axis=0, keepdims=True)
-            scores[here, :] = exponent
-            soft_grad[here, :] = gradient
-        inverse_sum = 1.0 / row_sum
-        delta = delta * inverse_sum
-        query_grad = jnp.zeros((2 * TILE, DIM), f32)
-        for t in range(SPAN // TILE):
-            here = pl.ds(t * TILE, TILE)
-            there = pl.ds(pl.multiple_of(base + t * TILE, TILE), TILE)
-            softmax = scores[here, :] * inverse_sum
-            grad_scores = (softmax * (soft_grad[here, :] - delta)).astype(bf16)
-            acc_v[j, there, :] += lax.dot_general(
-                softmax.astype(bf16), out_grad, nn, preferred_element_type=f32
-            )
-            acc_k[j, there, :] += lax.dot_general(
-                grad_scores, q, nn, preferred_element_type=f32
-            )
-            query_grad += lax.dot_general(
-                grad_scores, khat[there, :], tn, preferred_element_type=f32
-            )
+            scores[g, here(t), :] = tile
+            row_max[g] = jnp.maximum(row_max[g], jnp.max(tile, axis=0, keepdims=True))
+
+        def gradient_tile(g, t):
+            soft_grad[g, here(t), :] = lax.dot_general(
+                vcat[j, there(t), :], out_grad[g], nt, preferred_element_type=f32
+            )
+
+        def exponent_tile(g, t):
+            exponent = jnp.exp2(scores[g, here(t), :] * exp2_scale - row_max[g])
+            row_sum[g] = row_sum[g] + jnp.sum(exponent, axis=0, keepdims=True)
+            delta[g] = delta[g] + jnp.sum(
+                exponent * soft_grad[g, here(t), :], axis=0, keepdims=True
+            )
+            scores[g, here(t), :] = exponent
+
+        def product_tile(g, t):
+            softmax = scores[g, here(t), :] * row_sum[g]
+            grad_scores = (softmax * (soft_grad[g, here(t), :] - delta[g])).astype(bf16)
+            acc_v[j, there(t), :] += lax.dot_general(
+                softmax.astype(bf16), out_grad[g], nn, preferred_element_type=f32
+            )
+            acc_k[j, there(t), :] += lax.dot_general(
+                grad_scores, q[g], nn, preferred_element_type=f32
+            )
+            query_grad[g] = query_grad[g] + lax.dot_general(
+                khat[there(t), :], grad_scores, tn, preferred_element_type=f32
+            )
+
+        def close_max(g):
+            row_max[g] = row_max[g] * exp2_scale
+
+        def close_sum(g):
+            row_sum[g] = 1.0 / row_sum[g]
+            delta[g] = delta[g] * row_sum[g]
+
+        for t in range(tiles):
+            score_tile(0, t)
+        for t in range(tiles):
+            gradient_tile(0, t)
+        close_max(0)
+        for t in range(tiles):
+            score_tile(1, t)
+            exponent_tile(0, t)
+        close_max(1)
+        close_sum(0)
+        for t in range(tiles):
+            gradient_tile(1, t)
+            product_tile(0, t)
+            exponent_tile(1, t)
+        close_sum(1)
+        for t in range(tiles):
+            product_tile(1, t)
         for g in range(2):
             head_columns = pl.ds(pl.multiple_of((2 * j + g) * DIM, DIM), DIM)
             part = pl.ds(g * TILE, TILE)
-            grad = query_grad[g * TILE : (g + 1) * TILE] * score_scale
+            grad = query_grad[g].T * score_scale
             turned = grad * cos_table[mine, :] - half_turn(grad) * sin_table[mine, :]
             unit = qunit[part, :]
             gain_acc[0] += fold_rows(turned * unit)
             weighted = turned * query_gain[...]
             mean = jnp.mean(weighted * unit, axis=-1, keepdims=True)
             dq_all[rows, head_columns] = (qinv[part, :] * (weighted - unit * mean)).astype(bf16)
-
-    def dq_copy(j):
-        return pltpu.make_async_copy(
-            dq_all.at[:, columns(j, 2 * DIM)], dq_hbm.at[:, columns(j, 2 * DIM)], out_sem.at[j, 0]
-        )
-
-    def dk_copy(j):
-        return pltpu.make_async_copy(
-            dk_all.at[:, columns(j)], dk_hbm.at[:, columns(j)], out_sem.at[j, 1]
-        )
-
-    def dv_copy(j):
-        return pltpu.make_async_copy(
-            dv_all.at[:, columns(j)], dv_hbm.at[:, columns(j)], out_sem.at[j, 2]
-        )
 
     def hand_on(j):
         for n, (copy, onward, acc) in enumerate(
@@ -387,7 +403,6 @@
             return carry
 
         lax.fori_loop(0, ROWS // TILE, key_step, 0)
-        dk_copy(j).start()
         value_copy.wait_recv()
 
         def value_step(n, carry):
@@ -399,27 +414,40 @@
             return carry
 
         lax.fori_loop(0, ROWS // TILE, value_step, 0)
-        dv_copy(j).start()
+
+    def between(j):
+        @pl.when(j == 0)
+        def _():
+            relay(1, 1)
+            start_own(2, 1)
+            start_own(3, 0)
+
+        @pl.when(j == 1)
+        def _():
+            relay(2, 1)
+            start_own(3, 1)
+            hand_on(0)
+
+        @pl.when(j == 2)
+        def _():
+            relay(3, 1)
+            finish(0)
 
     def head_step(j, carry):
         key_norm(j, ROWS, 2 * ROWS)
         acc_k[j] = jnp.zeros((KEYS, DIM), f32)
         acc_v[j] = jnp.zeros((KEYS, DIM), f32)
-
-        @pl.when(j < HEADS - 1)
-        def _():
-            relay(j + 1)
-
-        @pl.when(j < HEADS - 3)
-        def _():
-            start_own(j + 3)
-
         for copy in relay_copies(j):
             copy.wait_recv()
         key_norm(j, 0, ROWS)
 
         def row_step(i, inner):
             attend(j, i)
+
+            @pl.when(i == 0)
+            def _():
+                between(j)
+
             return inner
 
         lax.fori_loop(0, ROWS // TILE, row_step, 0)
@@ -427,7 +455,10 @@
         far_send[j, 1] = acc_v[j, pl.ds(0, ROWS), :].astype(bf16)
         for copy in far_copies(j):
             copy.start()
-        dq_copy(j).start()
+
+        @pl.when(j < 2)
+        def _():
+            relay(j + 2, 0)
 
         def gain_step(n, inner):
             here = pl.ds(pl.multiple_of(n * TILE, TILE), TILE)
@@ -438,13 +469,9 @@
 
         lax.fori_loop(0, KEYS // TILE, gain_step, 0)
 
-        @pl.when(j >= 1)
+        @pl.when(j == 2)
         def _():
-            hand_on(j - 1)
-
-        @pl.when(j >= 2)
-        def _():
-            finish(j - 2)
+            hand_on(1)
 
         return carry
 
@@ -495,12 +522,16 @@
         jnp.sum(gain_acc[1], axis=0, keepdims=True),
     )
     start_sum(0, spread)
-    hand_on(HEADS - 1)
+    hand_on(2)
+    finish(1)
     start_sum(1, end_sum(0))
-    finish(HEADS - 2)
+    hand_on(3)
     start_sum(2, end_sum(1))
-    gain_out[...] = end_sum(2)
-    finish(HEADS - 1)
+    finish(2)
+    gains = end_sum(2)
+    query_gain_out[...] = gains[0:1]
+    key_gain_out[...] = gains[1:2]
+    finish(3)
 
     for n, (size, mine, place) in enumerate(stages):
         for k in range(1, size):
@@ -510,9 +541,6 @@
         for copies in (own_copies(j), relay_copies(j), far_copies(j), near_copies(j)):
             for copy in copies:
                 copy.wait_send()
-        dq_copy(j).wait()
-        dk_copy(j).wait()
-        dv_copy(j).wait()
         return carry
 
     lax.fori_loop(0, HEADS, drain, 0)
@@ -526,19 +554,20 @@
         spacing = jnp.arange(DIM // 2, dtype=f32) * (2.0 / DIM)
         inverse_freq = 10000.0 ** (-spacing)
         inverse_freq = jnp.concatenate([inverse_freq, inverse_freq])[None]
-        hbm = pl.BlockSpec(memory_space=pl.ANY)
+        hbm = pl.BlockSpec(memory_space=pltpu.HBM)
         vmem = pl.BlockSpec(memory_space=pltpu.VMEM)
         smem = pl.BlockSpec(memory_space=pltpu.SMEM)
-        dq, dk, dv, gains = pl.pallas_call(
+        dq, dk, dv, dq_gain, dk_gain = pl.pallas_call(
             functools.partial(kernel, shards, heads),
             out_shape=(
-                jax.ShapeDtypeStruct(q.shape, bf16),
-                jax.ShapeDtypeStruct(k.shape, bf16),
-                jax.ShapeDtypeStruct(v.shape, bf16),
-                jax.ShapeDtypeStruct((8, DIM), f32),
+                pltpu.VMEM(q.shape, bf16),
+                pltpu.VMEM(k.shape, bf16),
+                pltpu.VMEM(v.shape, bf16),
+                pltpu.VMEM((1, DIM), f32),
+                pltpu.VMEM((1, DIM), f32),
             ),
             in_specs=[hbm] * 4 + [vmem] * 3 + [smem] * 2,
-            out_specs=(hbm, hbm, hbm, vmem),
+            out_specs=(vmem,) * 5,
             scratch_shapes=[
                 pltpu.VMEM((HEADS, KEYS, DIM), bf16),
                 pltpu.VMEM((HEADS, KEYS, DIM), bf16),
@@ -552,27 +581,23 @@
                 pltpu.VMEM((2 * TILE, DIM), f32),
                 pltpu.VMEM((2 * TILE, DIM), f32),
                 pltpu.VMEM((2 * TILE, DIM), bf16),
-                pltpu.VMEM((SPAN, 2 * TILE), f32),
-                pltpu.VMEM((SPAN, 2 * TILE), f32),
+                pltpu.VMEM((2, SPAN, TILE), f32),
+                pltpu.VMEM((2, SPAN, TILE), f32),
                 pltpu.VMEM((HEADS, KEYS, DIM), f32),
                 pltpu.VMEM((HEADS, KEYS, DIM), f32),
                 pltpu.VMEM((HEADS, 2, ROWS, DIM), bf16),
                 pltpu.VMEM((HEADS, 2, ROWS, DIM), bf16),
                 pltpu.VMEM((HEADS, 2, ROWS, DIM), bf16),
                 pltpu.VMEM((HEADS, 2, ROWS, DIM), bf16),
-                pltpu.VMEM((ROWS, 2 * HEADS * DIM), bf16),
-                pltpu.VMEM((ROWS, HEADS * DIM), bf16),
-                pltpu.VMEM((ROWS, HEADS * DIM), bf16),
                 pltpu.VMEM((2, 8, DIM), f32),
                 pltpu.VMEM((3, 8, DIM), f32),
                 pltpu.VMEM((3, most, 8, DIM), f32),
                 pltpu.SemaphoreType.DMA((2 * HEADS + 2,)),
-                pltpu.SemaphoreType.DMA((HEADS, 3)),
             ]
             + [pltpu.SemaphoreType.DMA((HEADS, 2)) for _ in range(8)]
             + [pltpu.SemaphoreType.DMA((3, most)) for _ in range(2)],
             compiler_params=pltpu.CompilerParams(
-                collective_id=0, has_side_effects=True, vmem_limit_bytes=60 * 1024 * 1024
+                collective_id=0, has_side_effects=True, vmem_limit_bytes=58 * 1024 * 1024
             ),
         )(
             q,
@@ -585,7 +610,7 @@
             doc_starts,
             windows,
         )
-        return dq, dk, dv, gains[0], gains[1]
+        return dq, dk, dv, dq_gain[0], dk_gain[0]
 
     split = P("seq", "head")
     return jax.shard_map(

time: 105 us -> 93.7 us (0.89); the launches traced: 105 us -> 92.3 us
  Pallas kernels: 98 us -> 87.5 us
  local copies, waits for them, and re-layouts: 5.62 us -> 3.58 us
    pallas_call x1, Pallas kernels: 98 us -> 87.5 us  [step(): pl.pallas_call(functools.partial(kernel, shards, heads), out_shape=(pltpu...]
    squeeze x1 -> x0, local copies, waits for them, and re-layouts: 1.28 us -> none  [step(): return (dq, dk, dv, gains[0], gains[1])]
    unnamed x7 -> x5, local copies, waits for them, and re-layouts: 4.35 us -> 3.58 us
where the time goes in v2:
time: 93.7 us; the launch traced here: 92.3 us
  Pallas kernels  87.5 us (93%)
  local copies, waits for them, and re-layouts  3.58 us (4%)
    pallas_call x1, Pallas kernels, step(): pl.pallas_call(functools.partial(kernel, shards, heads), out_shape=(pltpu...  87.5 us
    unnamed x5, local copies, waits for them, and re-layouts  3.58 us

profile of v2, /device:TPU:2, one launch (start us, length us, event | category | flops | bytes accessed | tf_op | source)
XLA Modules:
  0.0 92.3 jit_solution(6912280244724915265)
XLA Ops:
  0.6 0.6 maximum_bitcast_fusion.inverse_freq
  1.2 87.5 %shard_map.119 = (bf16[512,1024]{1,0:T(8,128)(2,1)S(1)}, bf16[512,512]{1,0:T(8,128)(2,1)S(1)}, bf16[512,512]{1,0:T(8,128)(2,1)S(1)}, f32[1,128]{1,0:T(1,128)S(1)}, f32[1,128]{1,0:T(1,128)S(1)}) custom-call(bf16[512,1024]{1,0:T(8,128)(2,1)} %q_hbm.1, bf16[512,512]{1,0:T(8,128)(2,1)} %k_hbm.1, bf16[512,512]{1,0:T(8,128)(2,1)} %v_hbm.1, ...), custom_call_target="tpu_custom_call" | custom-call | tf_op jit(solution)/shard_map/pallas_call | solution.py:560
  88.7 1.0 %copy.18 = bf16[512,1024]{1,0:T(8,128)(2,1)} copy(bf16[512,1024]{1,0:T(8,128)(2,1)S(1)} %get-tuple-element.15) | data formatting | bytes 2097152
  89.7 0.5 copy.21
  90.2 0.5 copy.22
  90.7 0.8 copy.19
  91.5 0.8 copy.20
  (1 shorter events, 0.0 us)
